TPU v7x, 32 devices: a whole 2x2x4 slice. The times are simulated.
32 devices in a mesh: grp: 8 (over z, core), dev: 4 (over y, x).
Axes of the slice: x: 2, y: 2, z: 4, core: 2. Of those that a mesh axis runs over, the one named last changes fastest.
Arguments:
- voxel_features: float32 [128, 64, 512], P(('grp', 'dev')), may hold values from -6 to 6
- fine_links: int32 [128, 26], P(('grp', 'dev')), may hold values from -1 to 127, as said below
- parent_codes: int32 [128], P(('grp', 'dev')), may hold values from 0 to 63, as said below
- coarse_links: int32 [64, 26], P(('grp', 'dev')), may hold values from -1 to 63, as said below
- fine_in_weight: float32 [64, 1728], replicated, may hold values from -0.15625 to 0.15625
- fine_in_bias: float32 [64], replicated, may hold values from -3 to 3
- down_weight: float32 [128, 64], replicated, may hold values from -0.75 to 0.75
- coarse_first_weight: float32 [128, 3456], replicated, may hold values from -0.109375 to 0.109375
- coarse_first_bias: float32 [128], replicated, may hold values from -3 to 3
- coarse_second_weight: float32 [128, 3456], replicated, may hold values from -0.109375 to 0.109375
- coarse_second_bias: float32 [128], replicated, may hold values from -3 to 3
- up_weight: float32 [64, 128], replicated, may hold values from -0.5 to 0.5
- fine_out_weight: float32 [64, 1728], replicated, may hold values from -0.15625 to 0.15625
- fine_out_bias: float32 [64], replicated, may hold values from -3 to 3
Outputs:
- refined: float32 [128, 64, 512], P(('grp', 'dev'))
Inputs may be any that keep to these rules, and one draw needn't show every extreme that they name: `fine_links`: devices are numbered along grp then dev, device d holding bricks d * 4 to (d + 1) * 4 - 1. An entry is -1 or a brick from d * 4 - 2 to (d + 1) * 4 + 1 for a brick of device d, with 2 = 2. parent_codes[i] = 8 * 2 * owner + 8 * slot + octant: owner is the dev index, within the brick's group of 4 devices, of the device that holds the parent, slot the parent's slot there (0 to 1), and octant = 4 * a + 2 * b + c the child's octant. Within a group all codes differ; the number of slots in use differs from device to device, and some device of every group uses all 2. `coarse_links`: device d holds slots d * 2 to (d + 1) * 2 - 1. An entry is -1 or a slot from (d - 1) * 2 to (d + 2) * 2 - 1 for a slot of device d.
All inputs are finite; a program needn't handle non-finite values.
Results may differ from a plain program's by a relative error of at most 0.0001.
Values sent between devices are 32-bit elements; how exact they have to be, the bound alone decides.
A program may use at most 128 MiB of HBM per device.

v0:
```python
import jax
import jax.numpy as jnp
from jax import lax
from jax.sharding import PartitionSpec as P

neighbour_offsets = [
    (step_x, step_y, step_z)
    for step_x in (-1, 0, 1)
    for step_y in (-1, 0, 1)
    for step_z in (-1, 0, 1)
    if (step_x, step_y, step_z) != (0, 0, 0)
]
source_planes = {-1: slice(7, 8), 0: slice(0, 8), 1: slice(0, 1)}


def extended(array, sides, width):
    for axis, dim in sides:
        count, length = (lax.axis_size(axis), array.shape[dim])
        up = [(i, (i + 1) % count) for i in range(count - 1)]
        down = [(j, i) for i, j in up]
        last = lax.slice_in_dim(array, length - width, length, axis=dim)
        initial = lax.slice_in_dim(array, 0, width, axis=dim)
        before = lax.ppermute(last, axis, up)
        after = lax.ppermute(initial, axis, down)
        array = jnp.concatenate([before, array, after], axis=dim)
    return array


def assemble(source, center, links):
    extent = source.shape[0]
    bricks = center.shape[0]
    channels = center.shape[1]
    bricks_ext = jnp.concatenate([source, jnp.zeros((1,) + source.shape[1:], source.dtype)], 0)
    bricks_ext = bricks_ext.reshape(extent + 1, channels, 8, 8, 8)
    picked = jnp.where(links < 0, extent, links)
    middle = center.reshape(bricks, channels, 8, 8, 8)
    slabs = []
    for step_x in (-1, 0, 1):
        rows = []
        for step_y in (-1, 0, 1):
            cells = []
            for step_z in (-1, 0, 1):
                if (step_x, step_y, step_z) == (0, 0, 0):
                    cells.append(middle)
                else:
                    column = neighbour_offsets.index((step_x, step_y, step_z))
                    planes = bricks_ext[
                        :, :, source_planes[step_x], source_planes[step_y], source_planes[step_z]
                    ]
                    cells.append(planes[picked[:, column]])
            rows.append(jnp.concatenate(cells, axis=4))
        slabs.append(jnp.concatenate(rows, axis=3))
    return jnp.concatenate(slabs, axis=2)


def convolve(source, center, links, weight, biases):
    padded = assemble(source, center, links)
    bricks = center.shape[0]
    channels = center.shape[1]
    summed = jnp.zeros((bricks, weight.shape[0], 512), jnp.float32)
    for offset_x in range(3):
        windows = []
        for offset_y in range(3):
            for offset_z in range(3):
                windows.append(
                    padded[
                        :,
                        :,
                        offset_x : offset_x + 8,
                        offset_y : offset_y + 8,
                        offset_z : offset_z + 8,
                    ].reshape(bricks, channels, 512)
                )
        stacked = jnp.concatenate(windows, axis=1)
        kernel = weight[:, 9 * offset_x * channels : (9 * offset_x + 9) * channels]
        summed = summed + jnp.einsum(
            "oc,bcv->bov", kernel, stacked, precision=lax.Precision.HIGHEST
        )
    return summed + biases[None, :, None]


def fine_conv(features, links, weight, biases, position):
    margin = features.shape[0] // 2
    grown = extended(features, ((("grp", "dev"), 0),), margin)
    local_links = jnp.where(links < 0, -1, links - (position * features.shape[0] - margin))
    return convolve(grown, features, local_links, weight, biases)


def coarse_conv(features, links, weight, biases, position):
    margin = features.shape[0]
    grown = extended(features, ((("grp", "dev"), 0),), margin)
    local_links = jnp.where(links < 0, -1, links - (position * features.shape[0] - margin))
    return convolve(grown, features, local_links, weight, biases)


def pooling(hidden):
    bricks = hidden.shape[0]
    channels = hidden.shape[1]
    return (
        hidden.reshape(bricks, channels, 4, 2, 4, 2, 4, 2)
        .sum(axis=(3, 5, 7))
        .reshape(bricks, channels * 64)
        * 0.125
    )


def octants_to_bricks(pieces, channels):
    slots = pieces.shape[0] // 8
    return (
        pieces.reshape(slots, 2, 2, 2, channels, 4, 4, 4)
        .transpose(0, 4, 1, 5, 2, 6, 3, 7)
        .reshape(slots, channels, 512)
    )


def bricks_to_octants(cubes, channels):
    slots = cubes.shape[0]
    return (
        cubes.reshape(slots, channels, 2, 4, 2, 4, 2, 4)
        .transpose(0, 2, 4, 6, 1, 3, 5, 7)
        .reshape(slots * 8, channels * 64)
    )


def upsample(octants, channels):
    bricks = octants.shape[0]
    grown = jnp.broadcast_to(
        octants.reshape(bricks, channels, 4, 1, 4, 1, 4, 1), (bricks, channels, 4, 2, 4, 2, 4, 2)
    )
    return grown.reshape(bricks, channels, 512)


def per_device(
    voxel_features,
    fine_links,
    parent_codes,
    coarse_links,
    fine_in_weight,
    fine_in_bias,
    down_weight,
    coarse_first_weight,
    coarse_first_bias,
    coarse_second_weight,
    coarse_second_bias,
    up_weight,
    fine_out_weight,
    fine_out_bias,
):
    channels = voxel_features.shape[1]
    slot_count = coarse_links.shape[0]
    position = lax.axis_index("grp") * lax.axis_size("dev") + lax.axis_index("dev")
    hidden = jax.nn.silu(
        fine_conv(voxel_features, fine_links, fine_in_weight, fine_in_bias, position)
    )
    pooled = pooling(hidden)
    code_start = lax.axis_index("dev") * (slot_count * 8)
    targets = code_start + jnp.arange(slot_count * 8, dtype=jnp.int32)
    as_float = parent_codes.astype(jnp.float32)
    segment = lax.all_gather(pooled, "dev", axis=0, tiled=True)
    code_rows = lax.all_gather(as_float, "dev", axis=0, tiled=True)
    onehot = (code_rows[None, :] == targets[:, None].astype(jnp.float32)).astype(jnp.float32)
    gathered = jnp.dot(
        onehot, segment, precision=lax.Precision.HIGHEST, preferred_element_type=jnp.float32
    )
    coarse_in = octants_to_bricks(gathered, channels)
    coarse_base = jnp.einsum("oc,bcv->bov", down_weight, coarse_in, precision=lax.Precision.HIGHEST)
    coarse_first = jax.nn.silu(
        coarse_conv(coarse_base, coarse_links, coarse_first_weight, coarse_first_bias, position)
    )
    coarse_second = jax.nn.silu(
        coarse_conv(coarse_first, coarse_links, coarse_second_weight, coarse_second_bias, position)
    )
    lifted = jnp.einsum("oc,bcv->bov", up_weight, coarse_second, precision=lax.Precision.HIGHEST)
    upward = bricks_to_octants(lifted, channels)
    segment = lax.all_gather(upward, "dev", axis=0, tiled=True)
    columns = jnp.arange(segment.shape[0], dtype=jnp.int32)
    onehot = (parent_codes[:, None] == columns[None, :]).astype(jnp.float32)
    rows_up = jnp.dot(
        onehot, segment, precision=lax.Precision.HIGHEST, preferred_element_type=jnp.float32
    )
    rising = upsample(rows_up, channels)
    blended = jax.nn.silu(hidden + rising)
    return voxel_features + fine_conv(blended, fine_links, fine_out_weight, fine_out_bias, position)


def solution(mesh):
    placed = (
        P(("grp", "dev"), None, None),
        P(("grp", "dev"), None),
        P(("grp", "dev")),
        P(("grp", "dev"), None),
        P(),
        P(),
        P(),
        P(),
        P(),
        P(),
        P(),
        P(),
        P(),
        P(),
    )
    return jax.shard_map(
        per_device,
        mesh=mesh,
        in_specs=placed,
        out_specs=P(("grp", "dev"), None, None),
        check_vma=False,
    )
```

profile of v0, /device:TPU:9, one launch (start us, length us, event | category | flops | bytes accessed | tf_op | source)
XLA Modules:
  0.0 618.9 jit_solution(3030708873751734856)
XLA Ops:
  7.6 4.6 collective-permute-start.1
  32.8 9.2 %all-reduce = f32[16]{0:T(128)} all-reduce(f32[16]{0:T(128)S(1)} %convert_dynamic-update-slice_fusion), channel_id=1, replica_groups=mesh['grp'=8,'dev'=4] {'dev'}, use_global_device_ids=true, to_apply=%add | all-reduce | flops 16 | bytes 128
  100.5 3.8 fusion.110
  125.6 4.5 fusion.117
  148.6 4.5 fusion.116
  192.7 5.7 fusion.37
  211.8 6.3 %all-gather = f32[4,4,4096]{2,1,0:T(4,128)S(1)} all-gather(f32[1,4,4096]{2,1,0:T(4,128)S(1)} %reshape.1980), channel_id=1, replica_groups=mesh['grp'=8,'dev'=4] {'dev'}, dimensions={0}, use_global_device_ids=true | all-gather | bytes 327680 | tf_op jit(solution)/shard_map/all_gather | solution.py:159
  218.6 13.1 %reshape.400 = f32[2,2,2,2,64,4,4,4]{7,6,5,4,3,2,1,0:T(4,128)} reshape(f32[16,4096]{1,0:T(8,128)S(1)} %fusion.48) | data formatting | bytes 524288 | tf_op jit(solution)/shard_map/reshape | solution.py:110
  231.8 7.1 %copy.314 = f32[2,64,2,4,2,4,2,4]{1,7,6,5,4,3,2,0:T(4,128)S(1)} copy(f32[2,64,2,4,2,4,2,4]{7,5,3,1,6,4,2,0:T(4,128)} %bitcast.622) | data formatting | bytes 524288 | tf_op jit(solution)/shard_map/transpose | solution.py:111
  239.4 7.0 %collective-permute-start.3 = (f32[2,128,512]{1,2,0:T(8,128)S(1)}, f32[2,128,512]{1,2,0:T(8,128)S(1)}, u32[]{:S(2)}, u32[]{:S(2)}) collective-permute-start(f32[2,128,512]{1,2,0:T(8,128)S(1)} %bitcast.643), channel_id=1, source_target_pairs={{1,0},{2,1},{3,2},{4,3},{5,4},{6,5},{7,6},{8,7},{9,8},{10,9},{11,1... | collective-permute-start | bytes 1572872 | tf_op jit(solution)/shard_map/ppermute | solution.py:24
  248.6 15.0 %collective-permute-done.3 = f32[2,128,512]{1,2,0:T(8,128)S(1)} collective-permute-done((f32[2,128,512]{1,2,0:T(8,128)S(1)}, f32[2,128,512]{1,2,0:T(8,128)S(1)}, u32[]{:S(2)}, u32[]{:S(2)}) %collective-permute-start.3) | collective-permute-done | bytes 524320 | tf_op jit(solution)/shard_map/ppermute | solution.py:24
  263.6 5.9 collective-permute-done.2
  301.1 4.0 fusion.15
  308.7 6.0 convolution_add_fusion.7
  315.4 4.0 divide_multiply_fusion.1
  321.3 3.8 collective-permute-start.4
  325.2 10.2 %collective-permute-done.5 = f32[2,128,512]{1,2,0:T(8,128)S(1)} collective-permute-done((f32[2,128,512]{1,2,0:T(8,128)S(1)}, f32[2,128,512]{1,2,0:T(8,128)S(1)}, u32[]{:S(2)}, u32[]{:S(2)}) %collective-permute-start.5) | collective-permute-done | bytes 524320 | tf_op jit(solution)/shard_map/ppermute | solution.py:24
  335.4 5.6 collective-permute-done.4
  373.0 4.1 fusion.11
  380.8 6.1 convolution_add_fusion.5
  387.5 4.1 fusion.6
  392.7 6.3 %copy.350 = f32[2,2,2,2,64,4,4,4]{7,6,5,4,3,2,1,0:T(4,128)} copy(f32[2,2,2,2,64,4,4,4]{4,7,3,6,2,5,1,0:T(4,128)S(1)} %bitcast.869) | data formatting | bytes 524288 | tf_op jit(solution)/shard_map/transpose | solution.py:120
  399.0 13.0 %reshape.459 = f32[16,4096]{1,0:T(8,128)} reshape(f32[2,2,2,2,64,4,4,4]{7,6,5,4,3,2,1,0:T(4,128)} %copy.350) | data formatting | bytes 524288 | tf_op jit(solution)/shard_map/reshape | solution.py:121
  412.0 27.7 %all-gather.3.cloned.1.call-done = f32[64,4096]{1,0:T(8,128)} async-done(((f32[16,4096]{1,0:T(8,128)}), f32[64,4096]{1,0:T(8,128)}) %all-gather.3.cloned.1.call-update) | async-done | bytes 1048592 | tf_op jit(solution)/shard_map/all_gather | solution.py:175
  446.4 3.8 collective-permute-start.7
  452.4 5.8 collective-permute-done.7
  458.2 4.6 collective-permute-done.6
  504.5 3.8 fusion.108
  529.6 4.5 fusion.113
  552.5 4.5 fusion.112
  596.6 5.6 fusion.33
  607.4 4.2 fusion.2
  (670 shorter events, 382.9 us)
Async XLA Ops:
  6.5 232.3 %copy-start = (f32[128,64]{0,1:T(8,128)S(1)}, f32[128,64]{0,1:T(8,128)}, u32[]{:S(2)}) copy-start(f32[128,64]{0,1:T(8,128)} %param.20) | copy-start | bytes 98308
  6.5 433.2 %all-gather.3.cloned.1.call-start = ((), (), s32[]{:S(2)}) async-start(), calls=%async_computation | async-start | bytes 1310720 | tf_op jit(solution)/shard_map/all_gather | solution.py:175
  7.6 37.9 %collective-permute-start.1 = (f32[2,64,512]{2,1,0:T(8,128)S(1)}, f32[2,64,512]{2,1,0:T(8,128)S(1)}, u32[]{:S(2)}, u32[]{:S(2)}) collective-permute-start(f32[2,64,512]{2,1,0:T(8,128)S(1)} %get-tuple-element.280), channel_id=1, source_target_pairs={{1,0},{2,1},{3,2},{4,3},{5,4},{6,5},{7,6},{8,7},{9,8},{10,9},{11,1... | collective-permute-start | bytes 786440 | tf_op jit(solution)/shard_map/ppermute | solution.py:24
  12.3 33.2 %collective-permute-start = (f32[2,64,512]{2,1,0:T(8,128)S(1)}, f32[2,64,512]{2,1,0:T(8,128)S(1)}, u32[]{:S(2)}, u32[]{:S(2)}) collective-permute-start(f32[2,64,512]{2,1,0:T(8,128)S(1)} %get-tuple-element.279), channel_id=1, source_target_pairs={{0,1},{1,2},{2,3},{3,4},{4,5},{5,6},{6,7},{7,8},{8,9},{9,10},{10,1... | collective-permute-start | bytes 786440 | tf_op jit(solution)/shard_map/ppermute | solution.py:23
  43.4 50.8 %copy-start.2 = (f32[4,64,512]{1,2,0:T(8,128)}, f32[4,64,512]{1,2,0:T(8,128)S(1)}, u32[]{:S(2)}) copy-start(f32[4,64,512]{1,2,0:T(8,128)S(1)} %copy.262) | copy-start | bytes 1572868
  72.0 12.1 %copy-start.68 = (f32[9,64,8]{1,2,0:T(8,128)S(1)}, f32[9,64,8]{1,2,0:T(8,128)}, u32[]{:S(2)}) copy-start(f32[9,64,8]{1,2,0:T(8,128)} %copy.259) | copy-start | bytes 55300
  132.5 12.9 %copy-start.4 = (f32[4,64,512]{2,1,0:T(8,128)S(1)}, f32[4,64,512]{2,1,0:T(8,128)}, u32[]{:S(2)}) copy-start(f32[4,64,512]{2,1,0:T(8,128)} %param.14) | copy-start | bytes 1572868
  180.5 17.9 %slice-start.8 = ((s8[4718592]{0:T(1024)(128)(4,1)}), s8[524288]{0:T(1024)(128)(4,1)S(1)}, s32[]{:S(2)}) async-start(s8[4718592]{0:T(1024)(128)(4,1)} %bitcast.733), calls=%async_computation.9 | async-start | bytes 1048576
  206.9 11.4 %copy-start.98 = (f32[16]{0:T(128)S(1)}, f32[16]{0:T(128)}, u32[]{:S(2)}) copy-start(f32[16]{0:T(128)} %add_convert_fusion) | copy-start | bytes 196
  231.7 16.7 %copy-start.91 = (s32[2]{0:T(128)S(1)}, s32[2]{0:T(128)}, u32[]{:S(2)}) copy-start(s32[2]{0:T(128)} %get-tuple-element.50) | copy-start | bytes 28
  231.7 16.7 %copy-start.92 = (s32[2]{0:T(128)S(1)}, s32[2]{0:T(128)}, u32[]{:S(2)}) copy-start(s32[2]{0:T(128)} %get-tuple-element.56) | copy-start | bytes 28
  231.7 16.8 %copy-start.89 = (s32[2]{0:T(128)S(1)}, s32[2]{0:T(128)}, u32[]{:S(2)}) copy-start(s32[2]{0:T(128)} %get-tuple-element.32) | copy-start | bytes 28
  231.7 16.8 %copy-start.90 = (s32[2]{0:T(128)S(1)}, s32[2]{0:T(128)}, u32[]{:S(2)}) copy-start(s32[2]{0:T(128)} %get-tuple-element.33) | copy-start | bytes 28
  231.7 16.8 %copy-start.87 = (s32[2]{0:T(128)S(1)}, s32[2]{0:T(128)}, u32[]{:S(2)}) copy-start(s32[2]{0:T(128)} %get-tuple-element.34) | copy-start | bytes 28
  231.7 16.8 %copy-start.88 = (s32[2]{0:T(128)S(1)}, s32[2]{0:T(128)}, u32[]{:S(2)}) copy-start(s32[2]{0:T(128)} %get-tuple-element.35) | copy-start | bytes 28
  231.7 16.8 %copy-start.85 = (s32[2]{0:T(128)S(1)}, s32[2]{0:T(128)}, u32[]{:S(2)}) copy-start(s32[2]{0:T(128)} %get-tuple-element.36) | copy-start | bytes 28
  231.7 16.8 %copy-start.86 = (s32[2]{0:T(128)S(1)}, s32[2]{0:T(128)}, u32[]{:S(2)}) copy-start(s32[2]{0:T(128)} %get-tuple-element.37) | copy-start | bytes 28
  231.7 16.8 %copy-start.83 = (s32[2]{0:T(128)S(1)}, s32[2]{0:T(128)}, u32[]{:S(2)}) copy-start(s32[2]{0:T(128)} %get-tuple-element.38) | copy-start | bytes 28
  231.7 16.8 %copy-start.84 = (s32[2]{0:T(128)S(1)}, s32[2]{0:T(128)}, u32[]{:S(2)}) copy-start(s32[2]{0:T(128)} %get-tuple-element.39) | copy-start | bytes 28
  231.7 37.7 %copy-start.82 = (f32[7]{0:T(128)S(1)}, f32[7]{0:T(128)}, u32[]{:S(2)}) copy-start(f32[7]{0:T(128)} %pad.165.clone) | copy-start | bytes 88
  239.4 24.1 %collective-permute-start.3 = (f32[2,128,512]{1,2,0:T(8,128)S(1)}, f32[2,128,512]{1,2,0:T(8,128)S(1)}, u32[]{:S(2)}, u32[]{:S(2)}) collective-permute-start(f32[2,128,512]{1,2,0:T(8,128)S(1)} %bitcast.643), channel_id=1, source_target_pairs={{1,0},{2,1},{3,2},{4,3},{5,4},{6,5},{7,6},{8,7},{9,8},{10,9},{11,1... | collective-permute-start | bytes 1572872 | tf_op jit(solution)/shard_map/ppermute | solution.py:24
  246.5 23.0 %collective-permute-start.2 = (f32[2,128,512]{1,2,0:T(8,128)S(1)}, f32[2,128,512]{1,2,0:T(8,128)S(1)}, u32[]{:S(2)}, u32[]{:S(2)}) collective-permute-start(f32[2,128,512]{1,2,0:T(8,128)S(1)} %bitcast.644), channel_id=1, source_target_pairs={{0,1},{1,2},{2,3},{3,4},{4,5},{5,6},{6,7},{7,8},{8,9},{9,10},{10,1... | collective-permute-start | bytes 1572872 | tf_op jit(solution)/shard_map/ppermute | solution.py:23
  319.4 16.0 %collective-permute-start.5 = (f32[2,128,512]{1,2,0:T(8,128)S(1)}, f32[2,128,512]{1,2,0:T(8,128)S(1)}, u32[]{:S(2)}, u32[]{:S(2)}) collective-permute-start(f32[2,128,512]{1,2,0:T(8,128)S(1)} %divide_multiply_fusion.1), channel_id=1, source_target_pairs={{1,0},{2,1},{3,2},{4,3},{5,4},{6,5},{7,6},{8,7},{9,8},{10,9},{11,1... | collective-permute-start | bytes 1572872 | tf_op jit(solution)/shard_map/ppermute | solution.py:24
  321.3 19.6 %collective-permute-start.4 = (f32[2,128,512]{1,2,0:T(8,128)S(1)}, f32[2,128,512]{1,2,0:T(8,128)S(1)}, u32[]{:S(2)}, u32[]{:S(2)}) collective-permute-start(f32[2,128,512]{1,2,0:T(8,128)S(1)} %divide_multiply_fusion.1), channel_id=1, source_target_pairs={{0,1},{1,2},{2,3},{3,4},{4,5},{5,6},{6,7},{7,8},{8,9},{9,10},{10,1... | collective-permute-start | bytes 1572872 | tf_op jit(solution)/shard_map/ppermute | solution.py:23
  399.0 40.7 %copy-start.96 = (s32[4]{0:T(128)S(1)}, s32[4]{0:T(128)}, u32[]{:S(2)}) copy-start(s32[4]{0:T(128)} %param.16) | copy-start | bytes 52
  444.2 18.6 %copy-start.81 = (f32[9]{0:T(128)S(1)}, f32[9]{0:T(128)}, u32[]{:S(2)}) copy-start(f32[9]{0:T(128)} %copy-done.80) | copy-start | bytes 112
  446.3 20.5 %copy-start.6 = (f32[4,64,512]{2,1,0:T(8,128)}, f32[4,64,512]{2,1,0:T(8,128)S(1)}, u32[]{:S(2)}) copy-start(f32[4,64,512]{2,1,0:T(8,128)S(1)} %divide_multiply_fusion) | copy-start | bytes 1572868
  446.4 11.9 %collective-permute-start.7 = (f32[2,64,512]{2,1,0:T(8,128)S(1)}, f32[2,64,512]{2,1,0:T(8,128)S(1)}, u32[]{:S(2)}, u32[]{:S(2)}) collective-permute-start(f32[2,64,512]{2,1,0:T(8,128)S(1)} %get-tuple-element.274), channel_id=1, source_target_pairs={{1,0},{2,1},{3,2},{4,3},{5,4},{6,5},{7,6},{8,7},{9,8},{10,9},{11,1... | collective-permute-start | bytes 786440 | tf_op jit(solution)/shard_map/ppermute | solution.py:24
  450.2 12.6 %collective-permute-start.6 = (f32[2,64,512]{2,1,0:T(8,128)S(1)}, f32[2,64,512]{2,1,0:T(8,128)S(1)}, u32[]{:S(2)}, u32[]{:S(2)}) collective-permute-start(f32[2,64,512]{2,1,0:T(8,128)S(1)} %get-tuple-element.273), channel_id=1, source_target_pairs={{0,1},{1,2},{2,3},{3,4},{4,5},{5,6},{6,7},{7,8},{8,9},{9,10},{10,1... | collective-permute-start | bytes 786440 | tf_op jit(solution)/shard_map/ppermute | solution.py:23
  452.4 45.8 %copy-start.3 = (f32[4,64,512]{1,2,0:T(8,128)}, f32[4,64,512]{1,2,0:T(8,128)S(1)}, u32[]{:S(2)}) copy-start(f32[4,64,512]{1,2,0:T(8,128)S(1)} %copy.367) | copy-start | bytes 1572868
  536.5 12.8 %copy-start.7 = (f32[4,64,512]{2,1,0:T(8,128)S(1)}, f32[4,64,512]{2,1,0:T(8,128)}, u32[]{:S(2)}) copy-start(f32[4,64,512]{2,1,0:T(8,128)} %copy-done.6) | copy-start | bytes 1572868
  584.4 17.8 %slice-start.10 = ((s8[4718592]{0:T(1024)(128)(4,1)}), s8[524288]{0:T(1024)(128)(4,1)S(1)}, s32[]{:S(2)}) async-start(s8[4718592]{0:T(1024)(128)(4,1)} %bitcast.735), calls=%async_computation.11 | async-start | bytes 1048576
  (90 other events, 467.9 us)
Sparse Core Ops, SparseCore 0:
  412.1 27.5 all-gather.2
where the time goes:
time: 629 us; the launch traced here: 619 us
  local copies, waits for them, and re-layouts  385 us (61%)
  waiting for transfers between devices  74.8 us (12%)
  matrix products  57.5 us (9%)
  other arithmetic  41.5 us (7%)
  starting transfers between devices  27 us (4%)
  between operations  17.5 us (3%)
  blocking collectives  15.6 us (2%)
    reshape x52, local copies, waits for them, and re-layouts, convolve(): windows.append(padded[:, :, offset_x:offset_x + 8, offset_y:offset_y + 8,...  111 us
    gather x104, local copies, waits for them, and re-layouts, assemble(): cells.append(planes[picked[:, column]])  77.7 us
    unnamed x343, local copies, waits for them, and re-layouts  69.8 us
    dot_general x12, matrix products, convolve(): jnp.einsum('oc,bcv->bov', kernel, stacked, precision=lax.Precision.HIGHEST)  54.1 us
    slice x16, local copies, waits for them, and re-layouts, convolve(): padded[:, :, offset_x:offset_x + 8, offset_y:offset_y + 8, offset_z:offse...  40.5 us
    ppermute x4, waiting for transfers between devices, extended(): after = lax.ppermute(initial, axis, down)  31 us
    all_gather x1, waiting for transfers between devices, per_device(): segment = lax.all_gather(upward, 'dev', axis=0, tiled=True)  27.7 us
    slice x46, local copies, waits for them, and re-layouts, assemble(): bricks_ext[:, :, source_planes[step_x], source_planes[step_y], source_pla...  24.9 us
  transfers between devices with their start and end apart: 9, of which 7 were waited for; matrix products, arithmetic and copies ran while one was open for 4% of the time, Pallas kernels for 0%

commit v1 on v0

v1 whole, which is shorter than its diff:
```python
import functools

import jax
import jax.numpy as jnp
from jax import lax
from jax.experimental import pallas as pl
from jax.experimental.pallas import tpu as pltpu
from jax.sharding import PartitionSpec as P

F32 = jnp.float32
BF16 = jnp.bfloat16
MESH = pl.DeviceIdType.MESH
SIDE = 8
VOX = SIDE * SIDE * SIDE
OCT = VOX // 8
PADDED = SIDE + 2
HALO = 2
LIMIT = 60 * 1024 * 1024

offsets = [(x, y, z) for x in (-1, 0, 1) for y in (-1, 0, 1) for z in (-1, 0, 1)]
columns = {o: k for k, o in enumerate(o for o in offsets if o != (0, 0, 0))}
source = {-1: slice(7, 8), 0: slice(0, 8), 1: slice(0, 1)}
target = {-1: slice(0, 1), 0: slice(1, 9), 1: slice(9, 10)}


def split(v):
    high = v.astype(BF16).astype(F32)
    return high, v - high


def silu(v):
    return v / (1.0 + jnp.exp(-v))


def product(a, b, dims=((1,), (1,))):
    return lax.dot_general(a, b, (dims, ((), ())), preferred_element_type=F32)


def precise(a, b, dims=((1,), (1,))):
    return lax.dot_general(
        a, b, (dims, ((), ())), preferred_element_type=F32, precision=lax.Precision.HIGHEST
    )


def spread(v):
    half = v.shape[0] // 2
    return jnp.concatenate([v[:half], v[half:]], axis=1)


def unspread(v):
    width = v.shape[1] // 2
    return jnp.concatenate([v[:, :width], v[:, width:]], axis=0)


def put_parts(parts, index, v):
    high, low = split(v)
    parts[index] = jnp.concatenate([high, low], axis=1).reshape(SIDE, SIDE, SIDE, 2 * v.shape[1])


def fill(parts, own, start, links, brick, padded):
    for dx, dy, dz in offsets:
        spot = (dz + 1, target[dx], target[dy])
        if (dx, dy, dz) == (0, 0, 0):
            padded[spot] = parts[own]
            continue
        link = links[brick, columns[dx, dy, dz]]
        found = link >= 0
        row = jnp.where(found, link - start, own)
        keep = jnp.where(found, 1.0, 0.0).astype(F32)
        padded[spot] = parts[row, source[dx], source[dy]] * keep


def unfold(padded, patches):
    width = padded.shape[-1]
    z_at = lax.broadcasted_iota(jnp.int32, (PADDED, SIDE, width), 1)
    for x in range(PADDED):
        middle = padded[1, x]
        padded[0, x] = pltpu.roll(jnp.where(z_at == SIDE - 1, padded[0, x], middle), 1, 1)
        padded[2, x] = pltpu.roll(jnp.where(z_at == 0, padded[2, x], middle), SIDE - 1, 1)
    for i in range(3):
        for j in range(3):
            for k in range(3):
                tap = 9 * i + 3 * j + k
                window = padded[k, i : i + SIDE, j : j + SIDE].reshape(VOX, width)
                patches[:, tap * width : (tap + 1) * width] = window.astype(BF16)


def fine_matrix(weight, matrix):
    channels = weight.shape[0]
    lane = lax.broadcasted_iota(jnp.int32, (channels, 2 * channels), 1)
    for pair in range(14):
        if pair < 13:
            tile = weight[:, pair * 2 * channels : (pair + 1) * 2 * channels]
            turned = pltpu.roll(tile, channels, 1)
            taps = [
                jnp.where(lane < channels, tile, turned),
                jnp.where(lane < channels, turned, tile),
            ]
        else:
            tile = weight[:, 26 * channels : 27 * channels]
            taps = [jnp.concatenate([tile, tile], axis=1)]
        for at, tap in enumerate(taps):
            high, low = split(tap)
            cols = slice((2 * pair + at) * 2 * channels, (2 * pair + at + 1) * 2 * channels)
            matrix[0:channels, cols] = high.astype(BF16)
            matrix[channels : 2 * channels, cols] = low.astype(BF16)


def coarse_matrix(weight, matrix):
    channels = weight.shape[0]
    for tap in range(27):
        high, low = split(weight[:, tap * channels : (tap + 1) * channels])
        for part in range(2):
            cols = slice((2 * tap + part) * channels, (2 * tap + part + 1) * channels)
            matrix[0:channels, cols] = high.astype(BF16)
            matrix[channels : 2 * channels, cols] = low.astype(BF16)


def convolved(parts, own, start, links, brick, padded, patches, matrix, bias):
    fill(parts, own, start, links, brick, padded)
    unfold(padded, patches)
    both = product(patches[...], matrix[...])
    channels = both.shape[1] // 2
    return both[:, :channels] + both[:, channels:] + bias[...]


def place():
    return lax.axis_index("grp"), lax.axis_index("dev"), lax.axis_size("grp"), lax.axis_size("dev")


def first_kernel(x, left, right, links, weight, bias, hidden, pooled, parts, padded, patches, matrix):
    group, member, _, members = place()
    count = x.shape[0]
    start = (group * members + member) * count - HALO
    for i in range(count):
        put_parts(parts, HALO + i, x[i].T)
    for i in range(HALO):
        put_parts(parts, i, left[i].T)
        put_parts(parts, HALO + count + i, right[i].T)
    fine_matrix(weight, matrix)
    row = lax.broadcasted_iota(jnp.int32, (OCT, VOX), 0)
    col = lax.broadcasted_iota(jnp.int32, (OCT, VOX), 1)
    cell = (col // 128) * 16 + (col // 16 % 4) * 4 + col // 2 % 4
    pooling = jnp.where(row == cell, 0.125, 0.0).astype(BF16)

    def step(i, carry):
        out = silu(
            convolved(parts, HALO + i, start, links, i, padded, patches, matrix, bias)
        )
        hidden[i] = spread(out)
        high, low = split(out)
        both = jnp.concatenate([high, low], axis=1).astype(BF16)
        sums = product(pooling, both, ((1,), (0,)))
        width = out.shape[1]
        pooled[i] = spread(sums[:, :width] + sums[:, width:])
        return carry

    lax.fori_loop(0, count, step, 0)


def octant_order(flip):
    row = lax.broadcasted_iota(jnp.int32, (VOX, VOX), 1 if flip else 0)
    col = lax.broadcasted_iota(jnp.int32, (VOX, VOX), 0 if flip else 1)
    x, y, z = row // 64, row // 8 % 8, row % 8
    spot = (x // 4 * 4 + y // 4 * 2 + z // 4) * 64 + x % 4 * 16 + y % 4 * 4 + z % 4
    return jnp.where(spot == col, 1.0, 0.0).astype(BF16)


def second_kernel(pooled, codes, links, down, weight, bias, first, pieces, parts, padded, patches, matrix):
    group, member, groups, members = place()
    slots = links.shape[0]
    count = pooled.shape[1]
    start = (group * members + member - 1) * slots
    position = group * members + member
    pieces[...] = jnp.zeros_like(pieces)
    coarse_matrix(weight, matrix)
    for near in range(3):
        there = position + near - 1
        there_group = (there + members) // members - 1
        there_member = there - there_group * members
        band = there_group - group + 1
        valid = (there >= 0) & (there < groups * members)
        for one in range(count):

            def visit(owner, carry):
                code = codes[(band * members + owner) * 8, one] - there_member * slots * 8

                @pl.when(valid & (code >= 0) & (code < slots * 8))
                def _():
                    pieces[near * slots * 8 + code] = unspread(
                        pooled[band * members + owner, one]
                    )

                return carry

            lax.fori_loop(0, members, visit, 0)
    order = octant_order(False)

    def base(slot, carry):
        piece = pieces[pl.ds(slot * 8, 8)].reshape(VOX, pieces.shape[-1])
        lifted = precise(piece, down[...])
        high, low = split(lifted)
        both = jnp.concatenate([high, low], axis=1).astype(BF16)
        parts[slot] = product(order, both, ((1,), (0,))).reshape(SIDE, SIDE, SIDE, both.shape[1])
        return carry

    lax.fori_loop(0, 3 * slots, base, 0)

    def step(i, carry):
        first[i] = silu(
            convolved(parts, slots + i, start, links, i, padded, patches, matrix, bias)
        )
        return carry

    lax.fori_loop(0, slots, step, 0)


def third_kernel(first, left, right, links, weight, bias, up, lifted, parts, padded, patches, matrix):
    group, member, _, members = place()
    slots = links.shape[0]
    start = (group * members + member - 1) * slots
    coarse_matrix(weight, matrix)
    for i in range(slots):
        put_parts(parts, i, left[i])
        put_parts(parts, slots + i, first[i])
        put_parts(parts, 2 * slots + i, right[i])
    order = octant_order(True)

    def step(i, carry):
        out = silu(
            convolved(parts, slots + i, start, links, i, padded, patches, matrix, bias)
        )
        high, low = split(precise(out, up[...]))
        both = jnp.concatenate([high, low], axis=1).astype(BF16)
        sums = product(order, both, ((1,), (0,)))
        width = high.shape[1]
        ordered = sums[:, :width] + sums[:, width:]
        for octant in range(8):
            lifted[i * 8 + octant] = spread(ordered[octant * OCT : (octant + 1) * OCT])
        return carry

    lax.fori_loop(0, slots, step, 0)


def fourth_kernel(x, hidden, left, right, lifted, codes, links, weight, bias, out, parts, padded, patches, matrix):
    group, member, groups, members = place()
    count = x.shape[0]
    start = (group * members + member) * count - HALO
    fine_matrix(weight, matrix)
    row = lax.broadcasted_iota(jnp.int32, (VOX, OCT), 0)
    col = lax.broadcasted_iota(jnp.int32, (VOX, OCT), 1)
    cell = (row // 128) * 16 + (row // 16 % 4) * 4 + row // 2 % 4
    repeat = jnp.where(col == cell, 1.0, 0.0).astype(BF16)
    octants = lifted.shape[1]
    for i in range(count + 2 * HALO):
        if i < HALO:
            before, one, held = -1, count - HALO + i, left[i]
        elif i < HALO + count:
            before, one, held = 0, i - HALO, hidden[i - HALO]
        else:
            before, one, held = 1, i - HALO - count, right[i - HALO - count]
        there = jnp.clip(group * members + member + before, 0, groups * members - 1)
        there_group = there // members
        there_member = there - there_group * members
        band = there_group - group + 1
        code = codes[(band * members + there_member) * 8, one]
        piece = unspread(lifted[band * members + code // octants, code % octants])
        high, low = split(piece)
        both = jnp.concatenate([high, low], axis=1).astype(BF16)
        sums = product(repeat, both, ((1,), (0,)))
        width = high.shape[1]
        put_parts(parts, i, silu(unspread(held) + sums[:, :width] + sums[:, width:]))

    def step(i, carry):
        conv = convolved(parts, HALO + i, start, links, i, padded, patches, matrix, bias)
        out[i] = x[i] + conv.T
        return carry

    lax.fori_loop(0, count, step, 0)


def exchange_kernel(margins, shared, *refs):
    halos = len(margins)
    total = halos + shared
    ins, outs = refs[:total], refs[total : total + 2 * halos + shared]
    send_halo, recv_halo, send_all, recv_all = refs[total + 2 * halos + shared :]
    group, member, groups, members = place()
    position = group * members + member
    whole = groups * members
    has_left, has_right = position > 0, position < whole - 1
    has_low, has_high = group > 0, group < groups - 1
    left_at = (jnp.maximum(position - 1, 0) // members, (position + members - 1) % members)
    right_at = (jnp.minimum(position + 1, whole - 1) // members, (position + 1) % members)
    low_at = (jnp.maximum(group - 1, 0), members - 1)
    high_at = (jnp.minimum(group + 1, groups - 1), 0)

    barrier = pltpu.get_barrier_semaphore()

    def greet(where):
        pl.semaphore_signal(barrier, inc=1, device_id=where, device_id_type=MESH)

    count = jnp.int32(0)
    if halos:
        pl.when(has_left)(lambda: greet(left_at))
        pl.when(has_right)(lambda: greet(right_at))
        count = count + jnp.where(has_left, 1, 0) + jnp.where(has_right, 1, 0)
    if shared:
        for k in range(1, members):
            greet((group, (member + k) % members))
        for k in range(members):
            pl.when((member == 0) & has_low)(lambda k=k: greet((low_at[0], k)))
            pl.when((member == members - 1) & has_high)(lambda k=k: greet((high_at[0], k)))
        count = count + (members - 1) + jnp.where(has_low, 1, 0) + jnp.where(has_high, 1, 0)
    pl.semaphore_wait(barrier, count)

    def remote(src, dst, send, recv, where):
        return pltpu.make_async_remote_copy(
            src_ref=src, dst_ref=dst, send_sem=send, recv_sem=recv,
            device_id=where, device_id_type=MESH,
        )

    def each(action):
        for a in range(shared):
            src, out = ins[halos + a], outs[2 * halos + a]
            for k in range(1, members):
                spot = members + (member if action == "start" else (member + k) % members)
                copy = remote(
                    src, out.at[spot], send_all.at[a, k], recv_all.at[a, spot],
                    (group, (member + k) % members),
                )
                copy.start() if action == "start" else copy.wait()

            def across(where, base, lane, a=a, src=src, out=out):
                remote(
                    src, out.at[base + member], send_all.at[a, lane],
                    recv_all.at[a, base + member], where,
                ).start()

            def ended(where, lane, a=a, src=src, out=out):
                remote(
                    src, out.at[member], send_all.at[a, lane], recv_all.at[a, member], where
                ).wait_send()

            def arrived(spot, where, a=a, src=src, out=out):
                remote(
                    src, out.at[spot], send_all.at[a, 0], recv_all.at[a, spot], where
                ).wait_recv()

            if action == "start":
                pl.when(has_high)(lambda: across(high_at, 0, 0))
                pl.when(has_low)(lambda: across(low_at, 2 * members, members))
            else:
                pl.when(has_high)(lambda: ended(high_at, 0))
                pl.when(has_low)(lambda: ended(low_at, members))
                for k in range(members):
                    pl.when((member == 0) & has_low)(lambda k=k: arrived(k, low_at))
                    pl.when((member == members - 1) & has_high)(
                        lambda k=k: arrived(2 * members + k, high_at)
                    )
        for a, margin in enumerate(margins):
            src, before, after = ins[a], outs[2 * a], outs[2 * a + 1]
            length = src.shape[0]
            to_right = remote(
                src.at[length - margin : length], before, send_halo.at[a, 0],
                recv_halo.at[a, 0], right_at,
            )
            to_left = remote(
                src.at[0:margin], after, send_halo.at[a, 1], recv_halo.at[a, 1], left_at
            )
            if action == "start":
                pl.when(has_right)(to_right.start)
                pl.when(has_left)(to_left.start)
            else:
                pl.when(has_right)(to_right.wait_send)
                pl.when(has_left)(to_left.wait_send)
                pl.when(has_left)(to_right.wait_recv)
                pl.when(has_right)(to_left.wait_recv)

    each("start")
    for a in range(shared):
        outs[2 * halos + a][members + member] = ins[halos + a][...]
    each("wait")


def exchange(halos, shared, number):
    members = lax.axis_size("dev")
    shapes = []
    for array, margin in halos:
        shapes += [jax.ShapeDtypeStruct((margin,) + array.shape[1:], array.dtype)] * 2
    for array in shared:
        shapes.append(jax.ShapeDtypeStruct((3 * members,) + array.shape, array.dtype))
    total = len(halos) + len(shared)
    vmem = pl.BlockSpec(memory_space=pltpu.VMEM)
    halo_count, share_count = max(len(halos), 1), max(len(shared), 1)
    return pl.pallas_call(
        functools.partial(exchange_kernel, [m for _, m in halos], len(shared)),
        out_shape=shapes,
        in_specs=[vmem] * total,
        out_specs=[vmem] * len(shapes),
        scratch_shapes=[
            pltpu.SemaphoreType.DMA((halo_count, 2)),
            pltpu.SemaphoreType.DMA((halo_count, 2)),
            pltpu.SemaphoreType.DMA((share_count, members + 1)),
            pltpu.SemaphoreType.DMA((share_count, 3 * members)),
        ],
        name=f"exchange_{number}",
        compiler_params=pltpu.CompilerParams(
            collective_id=number, has_side_effects=True, vmem_limit_bytes=LIMIT
        ),
    )(*[a for a, _ in halos], *shared)


def local(kernel, shapes, args, scalars, scratch):
    vmem = pl.BlockSpec(memory_space=pltpu.VMEM)
    smem = pl.BlockSpec(memory_space=pltpu.SMEM)
    return pl.pallas_call(
        kernel,
        out_shape=shapes,
        in_specs=[smem if i in scalars else vmem for i in range(len(args))],
        out_specs=[vmem] * len(shapes),
        scratch_shapes=scratch,
        name=kernel.__name__,
        compiler_params=pltpu.CompilerParams(vmem_limit_bytes=LIMIT),
    )(*args)


def conv_scratch(bricks, channels):
    width = 2 * channels
    return [
        pltpu.VMEM((bricks, SIDE, SIDE, SIDE, width), F32),
        pltpu.VMEM((3, PADDED, PADDED, SIDE, width), F32),
        pltpu.VMEM((VOX, 27 * width), BF16),
        pltpu.VMEM((width, 27 * width), BF16),
    ]


def per_device(
    x, fine_links, parent_codes, coarse_links,
    in_weight, in_bias, down, one_weight, one_bias, two_weight, two_bias, up, out_weight, out_bias,
):
    count, channels = x.shape[0], x.shape[1]
    slots, wide = coarse_links.shape[0], one_bias.shape[0]
    sized = lambda *shape: jax.ShapeDtypeStruct(shape, F32)
    row = lambda bias: bias.reshape(1, -1)
    code_block = jnp.pad(parent_codes.reshape(1, -1), ((0, 7), (0, 128 - count)))
    left, right, codes = exchange([(x, HALO)], [code_block], 1)
    codes = codes.reshape(-1, 128)
    hidden, pooled = local(
        first_kernel,
        [sized(count, VOX // 2, 2 * channels), sized(count, OCT // 2, 2 * channels)],
        [x, left, right, fine_links, in_weight, row(in_bias)],
        (3,),
        conv_scratch(count + 2 * HALO, channels),
    )
    hidden_left, hidden_right, pooled = exchange([(hidden, HALO)], [pooled], 2)
    (first,) = local(
        second_kernel,
        [sized(slots, VOX, wide)],
        [pooled, codes, coarse_links, down, one_weight, row(one_bias)],
        (1, 2),
        [pltpu.VMEM((3 * slots * 8, OCT, channels), F32)] + conv_scratch(3 * slots, wide),
    )
    first_left, first_right = exchange([(first, slots)], [], 3)
    (lifted,) = local(
        third_kernel,
        [sized(slots * 8, OCT // 2, 2 * channels)],
        [first, first_left, first_right, coarse_links, two_weight, row(two_bias), up],
        (3,),
        conv_scratch(3 * slots, wide),
    )
    (lifted,) = exchange([], [lifted], 4)
    (out,) = local(
        fourth_kernel,
        [sized(count, channels, VOX)],
        [x, hidden, hidden_left, hidden_right, lifted, codes, fine_links, out_weight, row(out_bias)],
        (5, 6),
        conv_scratch(count + 2 * HALO, channels),
    )
    return out


def solution(mesh):
    bricks = P(("grp", "dev"), None, None)
    rows = P(("grp", "dev"), None)
    placed = (bricks, rows, P(("grp", "dev")), rows) + (P(),) * 10
    return jax.shard_map(
        per_device, mesh=mesh, in_specs=placed, out_specs=bricks, check_vma=False
    )
```

time: 629 us -> 146 us (0.23); the launches traced: 619 us -> 146 us
  local copies, waits for them, and re-layouts: 385 us -> 2.73 us
  Pallas kernels: 0 us -> 143 us
  waiting for transfers between devices: 74.8 us -> 0 us
  matrix products: 57.5 us -> 0 us
  other arithmetic: 41.5 us -> 0 us
  starting transfers between devices: 27 us -> 0 us
  between operations: 17.5 us -> 0.04 us
  blocking collectives: 15.6 us -> 0 us
    pallas_call x0 -> x8, Pallas kernels: none -> 143 us  [the longest x4 96.2 us: exchange(): pl.pallas_call(functools.partial(exchange_kernel, [m for _, m in halos],...]
    reshape x56 -> x0, local copies, waits for them, and re-layouts: 141 us -> none  [the longest x52 111 us: convolve(): windows.append(padded[:, :, offset_x:offset_x + 8, offset_y:offset_y + 8,...]
    gather x104 -> x0, local copies, waits for them, and re-layouts: 77.7 us -> none  [assemble(): cells.append(planes[picked[:, column]])]
    unnamed x343 -> x1, local copies, waits for them, and re-layouts: 69.8 us -> 1.47 us
    slice x64 -> x0, local copies, waits for them, and re-layouts: 66.5 us -> none  [the longest x16 40.5 us: convolve(): padded[:, :, offset_x:offset_x + 8, offset_y:offset_y + 8, offset_z:offse...]
    dot_general x16 -> x0, matrix products: 57.5 us -> none  [the longest x12 54.1 us: convolve(): jnp.einsum('oc,bcv->bov', kernel, stacked, precision=lax.Precision.HIGHEST)]
    ppermute x8 -> x0, waiting for transfers between devices: 47 us -> none  [the longest x4 31 us: extended(): after = lax.ppermute(initial, axis, down)]
    all_gather x1 -> x0, waiting for transfers between devices: 27.7 us -> none  [per_device(): segment = lax.all_gather(upward, 'dev', axis=0, tiled=True)]
  transfers between devices with their start and end apart: 9 -> 0, of which waited for: 7 -> 0; matrix products, arithmetic and copies ran while one was open for 4% -> 0% of each run, Pallas kernels for 0% -> 0%
where the time goes in v1:
time: 146 us
  Pallas kernels  143 us (98%)
  local copies, waits for them, and re-layouts  2.73 us (2%)
    pallas_call x4, Pallas kernels, exchange(): pl.pallas_call(functools.partial(exchange_kernel, [m for _, m in halos],...  96.2 us
    pallas_call x4, Pallas kernels, local(): pl.pallas_call(kernel, out_shape=shapes, in_specs=[smem if i in scalars e...  47 us

profile of v1, /device:TPU:9, one launch (start us, length us, event | category | flops | bytes accessed | tf_op | source)
XLA Modules:
  0.0 145.9 jit_solution(14344723884626235316)
XLA Ops:
  0.0 1.3 pad.4.refs_1_
  1.3 1.5 %copy.15.down = f32[128,64]{1,0:T(8,128)} copy(f32[128,64]{0,1:T(8,128)} %param.20) | data formatting | bytes 65536 | tf_op args[6]
  2.7 17.2 %exchange_1.1 = (f32[2,64,512]{2,1,0:T(8,128)}, f32[2,64,512]{2,1,0:T(8,128)}, s32[12,8,128]{2,1,0:T(8,128)}) custom-call(f32[4,64,512]{2,1,0:T(8,128)} %x.5, s32[8,128]{1,0:T(8,128)} %pad.4.refs_1_), custom_call_target="tpu_custom_call" | custom-call | tf_op jit(solution)/shard_map/exchange_1/pallas_call | solution.py:395
  19.9 10.5 %first_kernel.1 = (f32[4,256,128]{2,1,0:T(8,128)}, f32[4,32,128]{2,1,0:T(8,128)}) custom-call(f32[4,64,512]{2,1,0:T(8,128)} %x.5, f32[2,64,512]{2,1,0:T(8,128)} %get-tuple-element.15.left, f32[2,64,512]{2,1,0:T(8,128)} %get-tuple-element.16.right, s32[4,26]{1,0:T(4,128)} %links.7, f32[64,1728]{1,0:T(8,128)} %weight.4, f32[1,64]{1,0:T(1,128)} %bitcast.8), custom_call_target="tpu_custom_call" | custom-call | tf_op jit(solution)/shard_map/first_kernel/pallas_call | solution.py:416
  30.4 21.5 %exchange_2.1 = (f32[2,256,128]{2,1,0:T(8,128)}, f32[2,256,128]{2,1,0:T(8,128)}, f32[12,4,32,128]{3,2,1,0:T(8,128)}) custom-call(f32[4,256,128]{2,1,0:T(8,128)} %get-tuple-element.17.refs_0_.hidden, f32[4,32,128]{2,1,0:T(8,128)} %get-tuple-element.18.refs_1_), custom_call_target="tpu_custom_call" | custom-call | tf_op jit(solution)/shard_map/exchange_2/pallas_call | solution.py:395
  52.0 13.9 %second_kernel.1.refs_0_.first = f32[2,512,128]{2,1,0:T(8,128)} custom-call(f32[12,4,32,128]{3,2,1,0:T(8,128)} %get-tuple-element.21.pooled, s32[96,128]{1,0:T(8,128)} %bitcast.6, s32[2,26]{1,0:T(2,128)} %links.6, f32[128,64]{1,0:T(8,128)} %copy.15.down, f32[128,3456]{1,0:T(8,128)} %weight.5, f32[1,128]{1,0:T(1,128)} %bitcast.9), custom_call_target="tpu_custom_call" | custom-call | tf_op jit(solution)/shard_map/second_kernel/pallas_call | solution.py:416
  65.9 27.9 %exchange_3.1 = (f32[2,512,128]{2,1,0:T(8,128)}, f32[2,512,128]{2,1,0:T(8,128)}) custom-call(f32[2,512,128]{2,1,0:T(8,128)} %second_kernel.1.refs_0_.first), custom_call_target="tpu_custom_call" | custom-call | tf_op jit(solution)/shard_map/exchange_3/pallas_call | solution.py:395
  93.8 10.2 %third_kernel.1.refs_0_ = f32[16,32,128]{2,1,0:T(8,128)} custom-call(f32[2,512,128]{2,1,0:T(8,128)} %second_kernel.1.refs_0_.first, f32[2,512,128]{2,1,0:T(8,128)} %get-tuple-element.23.left, f32[2,512,128]{2,1,0:T(8,128)} %get-tuple-element.24.right, s32[2,26]{1,0:T(2,128)} %links.6, f32[128,3456]{1,0:T(8,128)} %weight.6, f32[1,128]{1,0:T(1,128)} %bitcast.10, ...), custom_call_target="tpu_custom_call" | custom-call | tf_op jit(solution)/shard_map/third_kernel/pallas_call | solution.py:416
  104.0 29.5 %exchange_4.1.lifted = f32[12,16,32,128]{3,2,1,0:T(8,128)} custom-call(f32[16,32,128]{2,1,0:T(8,128)} %third_kernel.1.refs_0_), custom_call_target="tpu_custom_call" | custom-call | tf_op jit(solution)/shard_map/exchange_4/pallas_call | solution.py:395
  133.6 12.3 %fourth_kernel.1 = f32[4,64,512]{2,1,0:T(8,128)} custom-call(f32[4,64,512]{2,1,0:T(8,128)} %x.5, f32[4,256,128]{2,1,0:T(8,128)} %get-tuple-element.17.refs_0_.hidden, f32[2,256,128]{2,1,0:T(8,128)} %get-tuple-element.19.left, f32[2,256,128]{2,1,0:T(8,128)} %get-tuple-element.20.right, f32[12,16,32,128]{3,2,1,0:T(8,128)} %exchange_4.1.lifted, ...), custom_call_target="tpu_custom_call" | custom-call | tf_op jit(solution)/shard_map/fourth_kernel/pallas_call | solution.py:416

commit v2 on v1

--- a/solution.py
+++ b/solution.py
@@ -15,6 +15,8 @@
 OCT = VOX // 8
 PADDED = SIDE + 2
 HALO = 2
+FINE_ROWS = 304
+COARSE_ROWS = 296
 LIMIT = 60 * 1024 * 1024
 
 offsets = [(x, y, z) for x in (-1, 0, 1) for y in (-1, 0, 1) for z in (-1, 0, 1)]
@@ -50,6 +52,42 @@
 def unspread(v):
     width = v.shape[1] // 2
     return jnp.concatenate([v[:, :width], v[:, width:]], axis=0)
+
+
+def surface_rank(p):
+    x, y, z = p // 64, p // 8 % 8, p % 8
+    inner = jnp.where(z == 0, 0, jnp.where(z == 7, 1, -1))
+    inner = jnp.where(inner < 0, -1, 224 + ((x - 1) * 6 + y - 1) * 2 + inner)
+    side = 128 + (x - 1) * 16 + z
+    edge = jnp.where(y == 0, side, jnp.where(y == 7, side + 8, inner))
+    return jnp.where(x == 0, p, jnp.where(x == 7, p - 384, edge))
+
+
+def surface_pick(rows):
+    rank = surface_rank(lax.broadcasted_iota(jnp.int32, (1, VOX), 1))
+    row = lax.broadcasted_iota(jnp.int32, (rows, VOX), 0)
+    return jnp.where(row == rank, 1.0, 0.0).astype(BF16)
+
+
+def surface_place(rows):
+    rank = surface_rank(lax.broadcasted_iota(jnp.int32, (VOX, rows), 0))
+    col = lax.broadcasted_iota(jnp.int32, (VOX, rows), 1)
+    return jnp.where(col == rank, 1.0, 0.0).astype(BF16)
+
+
+def both_parts(v):
+    high, low = split(v)
+    return jnp.concatenate([high, low], axis=1).astype(BF16)
+
+
+def joined(sums):
+    width = sums.shape[1] // 2
+    return sums[:, :width] + sums[:, width:]
+
+
+def put_surface(parts, index, placing, v):
+    sums = product(placing, both_parts(v), ((1,), (0,)))
+    parts[index] = sums.reshape(SIDE, SIDE, SIDE, sums.shape[1])
 
 
 def put_parts(parts, index, v):
@@ -128,15 +166,24 @@
     return lax.axis_index("grp"), lax.axis_index("dev"), lax.axis_size("grp"), lax.axis_size("dev")
 
 
-def first_kernel(x, left, right, links, weight, bias, hidden, pooled, parts, padded, patches, matrix):
+def pack_kernel(x, packed):
+    pick = surface_pick(FINE_ROWS)
+    for i in range(x.shape[0]):
+        high, low = split(x[i])
+        packed[i] = spread(product(pick, high.astype(BF16)) + product(pick, low.astype(BF16)))
+
+
+def first_kernel(x, left, right, links, weight, bias, hidden, packed, pooled, parts, padded, patches, matrix):
     group, member, _, members = place()
     count = x.shape[0]
     start = (group * members + member) * count - HALO
     for i in range(count):
         put_parts(parts, HALO + i, x[i].T)
+    placing = surface_place(FINE_ROWS)
     for i in range(HALO):
-        put_parts(parts, i, left[i].T)
-        put_parts(parts, HALO + count + i, right[i].T)
+        put_surface(parts, i, placing, unspread(left[i]))
+        put_surface(parts, HALO + count + i, placing, unspread(right[i]))
+    pick = surface_pick(FINE_ROWS)
     fine_matrix(weight, matrix)
     row = lax.broadcasted_iota(jnp.int32, (OCT, VOX), 0)
     col = lax.broadcasted_iota(jnp.int32, (OCT, VOX), 1)
@@ -148,11 +195,9 @@
             convolved(parts, HALO + i, start, links, i, padded, patches, matrix, bias)
         )
         hidden[i] = spread(out)
-        high, low = split(out)
-        both = jnp.concatenate([high, low], axis=1).astype(BF16)
-        sums = product(pooling, both, ((1,), (0,)))
-        width = out.shape[1]
-        pooled[i] = spread(sums[:, :width] + sums[:, width:])
+        both = both_parts(out)
+        pooled[i] = spread(joined(product(pooling, both, ((1,), (0,)))))
+        packed[i] = spread(joined(product(pick, both, ((1,), (0,)))))
         return carry
 
     lax.fori_loop(0, count, step, 0)
@@ -166,7 +211,7 @@
     return jnp.where(spot == col, 1.0, 0.0).astype(BF16)
 
 
-def second_kernel(pooled, codes, links, down, weight, bias, first, pieces, parts, padded, patches, matrix):
+def second_kernel(pooled, codes, links, down, weight, bias, first, packed, pieces, parts, padded, patches, matrix):
     group, member, groups, members = place()
     slots = links.shape[0]
     count = pooled.shape[1]
@@ -205,25 +250,29 @@
         return carry
 
     lax.fori_loop(0, 3 * slots, base, 0)
+    pick = surface_pick(COARSE_ROWS)
 
     def step(i, carry):
-        first[i] = silu(
+        out = silu(
             convolved(parts, slots + i, start, links, i, padded, patches, matrix, bias)
         )
+        first[i] = out
+        packed[i] = joined(product(pick, both_parts(out), ((1,), (0,))))
         return carry
 
     lax.fori_loop(0, slots, step, 0)
 
 
-def third_kernel(first, left, right, links, weight, bias, up, lifted, parts, padded, patches, matrix):
+def third_kernel(first, left, right, links, codes, weight, bias, up, wanted, lifted, parts, padded, patches, matrix):
     group, member, _, members = place()
     slots = links.shape[0]
     start = (group * members + member - 1) * slots
     coarse_matrix(weight, matrix)
+    placing = surface_place(COARSE_ROWS)
     for i in range(slots):
-        put_parts(parts, i, left[i])
+        put_surface(parts, i, placing, left[i])
         put_parts(parts, slots + i, first[i])
-        put_parts(parts, 2 * slots + i, right[i])
+        put_surface(parts, 2 * slots + i, placing, right[i])
     order = octant_order(True)
 
     def step(i, carry):
@@ -240,9 +289,23 @@
         return carry
 
     lax.fori_loop(0, slots, step, 0)
-
-
-def fourth_kernel(x, hidden, left, right, lifted, codes, links, weight, bias, out, parts, padded, patches, matrix):
+    bricks = wanted.shape[0] - 2 * HALO
+    each = bricks // members
+    zeros = jnp.zeros((HALO,) + wanted.shape[1:], F32)
+    wanted[0:HALO] = zeros
+    wanted[HALO + bricks :] = zeros
+
+    def choose(j, carry):
+        code = codes[(members + j // each) * 8, j % each] - member * slots * 8
+        mine = (code >= 0) & (code < slots * 8)
+        keep = jnp.where(mine, 1.0, 0.0).astype(F32)
+        wanted[HALO + j] = lifted[jnp.where(mine, code, 0)] * keep
+        return carry
+
+    lax.fori_loop(0, bricks, choose, 0)
+
+
+def fourth_kernel(x, hidden, left, right, window, low, high, links, weight, bias, out, parts, padded, patches, matrix):
     group, member, groups, members = place()
     count = x.shape[0]
     start = (group * members + member) * count - HALO
@@ -251,25 +314,33 @@
     col = lax.broadcasted_iota(jnp.int32, (VOX, OCT), 1)
     cell = (row // 128) * 16 + (row // 16 % 4) * 4 + row // 2 % 4
     repeat = jnp.where(col == cell, 1.0, 0.0).astype(BF16)
-    octants = lifted.shape[1]
+    placing = surface_place(FINE_ROWS)
     for i in range(count + 2 * HALO):
+        piece = window[0, i]
+        for owner in range(1, members):
+            piece = piece + window[owner, i]
         if i < HALO:
-            before, one, held = -1, count - HALO + i, left[i]
+            other = low[0, i]
+            for owner in range(1, members):
+                other = other + low[owner, i]
+            piece = jnp.where(member == 0, other, piece)
+        elif i >= HALO + count:
+            other = high[0, i - HALO - count]
+            for owner in range(1, members):
+                other = other + high[owner, i - HALO - count]
+            piece = jnp.where(member == members - 1, other, piece)
+        rising = joined(product(repeat, both_parts(unspread(piece)), ((1,), (0,))))
+        if i < HALO:
+            held = joined(
+                product(placing, both_parts(unspread(left[i])), ((1,), (0,)))
+            )
         elif i < HALO + count:
-            before, one, held = 0, i - HALO, hidden[i - HALO]
+            held = unspread(hidden[i - HALO])
         else:
-            before, one, held = 1, i - HALO - count, right[i - HALO - count]
-        there = jnp.clip(group * members + member + before, 0, groups * members - 1)
-        there_group = there // members
-        there_member = there - there_group * members
-        band = there_group - group + 1
-        code = codes[(band * members + there_member) * 8, one]
-        piece = unspread(lifted[band * members + code // octants, code % octants])
-        high, low = split(piece)
-        both = jnp.concatenate([high, low], axis=1).astype(BF16)
-        sums = product(repeat, both, ((1,), (0,)))
-        width = high.shape[1]
-        put_parts(parts, i, silu(unspread(held) + sums[:, :width] + sums[:, width:]))
+            held = joined(
+                product(placing, both_parts(unspread(right[i - HALO - count])), ((1,), (0,)))
+            )
+        put_parts(parts, i, silu(held + rising))
 
     def step(i, carry):
         conv = convolved(parts, HALO + i, start, links, i, padded, patches, matrix, bias)
@@ -279,11 +350,12 @@
     lax.fori_loop(0, count, step, 0)
 
 
-def exchange_kernel(margins, shared, *refs):
+def exchange_kernel(margins, shared, windows, *refs):
     halos = len(margins)
-    total = halos + shared
-    ins, outs = refs[:total], refs[total : total + 2 * halos + shared]
-    send_halo, recv_halo, send_all, recv_all = refs[total + 2 * halos + shared :]
+    total = halos + shared + windows
+    given = 2 * halos + shared + 3 * windows
+    ins, outs = refs[:total], refs[total : total + given]
+    send_halo, recv_halo, send_all, recv_all = refs[total + given :]
     group, member, groups, members = place()
     position = group * members + member
     whole = groups * members
@@ -304,7 +376,7 @@
         pl.when(has_left)(lambda: greet(left_at))
         pl.when(has_right)(lambda: greet(right_at))
         count = count + jnp.where(has_left, 1, 0) + jnp.where(has_right, 1, 0)
-    if shared:
+    if shared or windows:
         for k in range(1, members):
             greet((group, (member + k) % members))
         for k in range(members):
@@ -319,44 +391,57 @@
             device_id=where, device_id_type=MESH,
         )
 
+    def parts_of(a):
+        src = ins[halos + a]
+        if a < shared:
+            out = outs[2 * halos + a]
+            return (
+                lambda to: src, src, src,
+                lambda by: out.at[members + by],
+                lambda by: out.at[by],
+                lambda by: out.at[2 * members + by],
+            )
+        window, low, high = outs[2 * halos + shared + 3 * (a - shared) :][:3]
+        span = window.shape[1]
+        each = span - 2 * HALO
+        bricks = src.shape[0] - 2 * HALO
+        return (
+            lambda to: src.at[pl.ds(to * each, span)],
+            src.at[bricks : bricks + HALO],
+            src.at[HALO : 2 * HALO],
+            lambda by: window.at[by],
+            lambda by: low.at[by],
+            lambda by: high.at[by],
+        )
+
     def each(action):
-        for a in range(shared):
-            src, out = ins[halos + a], outs[2 * halos + a]
+        for a in range(shared + windows):
+            own, up, down, here, below, above = parts_of(a)
+            sends, recvs = send_all.at[a], recv_all.at[a]
             for k in range(1, members):
-                spot = members + (member if action == "start" else (member + k) % members)
+                other = (member + k) % members
+                by = member if action == "start" else other
                 copy = remote(
-                    src, out.at[spot], send_all.at[a, k], recv_all.at[a, spot],
-                    (group, (member + k) % members),
+                    own(other), here(by), sends.at[k], recvs.at[members + by], (group, other)
                 )
                 copy.start() if action == "start" else copy.wait()
-
-            def across(where, base, lane, a=a, src=src, out=out):
-                remote(
-                    src, out.at[base + member], send_all.at[a, lane],
-                    recv_all.at[a, base + member], where,
-                ).start()
-
-            def ended(where, lane, a=a, src=src, out=out):
-                remote(
-                    src, out.at[member], send_all.at[a, lane], recv_all.at[a, member], where
-                ).wait_send()
-
-            def arrived(spot, where, a=a, src=src, out=out):
-                remote(
-                    src, out.at[spot], send_all.at[a, 0], recv_all.at[a, spot], where
-                ).wait_recv()
-
+            to_high = remote(up, below(member), sends.at[0], recvs.at[member], high_at)
+            to_low = remote(
+                down, above(member), sends.at[members], recvs.at[2 * members + member], low_at
+            )
             if action == "start":
-                pl.when(has_high)(lambda: across(high_at, 0, 0))
-                pl.when(has_low)(lambda: across(low_at, 2 * members, members))
+                pl.when(has_high)(to_high.start)
+                pl.when(has_low)(to_low.start)
             else:
-                pl.when(has_high)(lambda: ended(high_at, 0))
-                pl.when(has_low)(lambda: ended(low_at, members))
+                pl.when(has_high)(to_high.wait_send)
+                pl.when(has_low)(to_low.wait_send)
                 for k in range(members):
-                    pl.when((member == 0) & has_low)(lambda k=k: arrived(k, low_at))
-                    pl.when((member == members - 1) & has_high)(
-                        lambda k=k: arrived(2 * members + k, high_at)
+                    from_low = remote(up, below(k), sends.at[0], recvs.at[k], low_at)
+                    from_high = remote(
+                        down, above(k), sends.at[0], recvs.at[2 * members + k], high_at
                     )
+                    pl.when((member == 0) & has_low)(from_low.wait_recv)
+                    pl.when((member == members - 1) & has_high)(from_high.wait_recv)
         for a, margin in enumerate(margins):
             src, before, after = ins[a], outs[2 * a], outs[2 * a + 1]
             length = src.shape[0]
@@ -379,21 +464,31 @@
     each("start")
     for a in range(shared):
         outs[2 * halos + a][members + member] = ins[halos + a][...]
+    for a in range(shared, shared + windows):
+        window, src = outs[2 * halos + shared + 3 * (a - shared)], ins[halos + a]
+        span = window.shape[1]
+        window[member] = src[pl.ds(member * (span - 2 * HALO), span)]
     each("wait")
 
 
-def exchange(halos, shared, number):
+def exchange(halos, shared, windows, number):
     members = lax.axis_size("dev")
     shapes = []
     for array, margin in halos:
         shapes += [jax.ShapeDtypeStruct((margin,) + array.shape[1:], array.dtype)] * 2
     for array in shared:
         shapes.append(jax.ShapeDtypeStruct((3 * members,) + array.shape, array.dtype))
-    total = len(halos) + len(shared)
+    for array in windows:
+        span = (array.shape[0] - 2 * HALO) // members + 2 * HALO
+        for rows in (span, HALO, HALO):
+            shapes.append(
+                jax.ShapeDtypeStruct((members, rows) + array.shape[1:], array.dtype)
+            )
+    total = len(halos) + len(shared) + len(windows)
     vmem = pl.BlockSpec(memory_space=pltpu.VMEM)
-    halo_count, share_count = max(len(halos), 1), max(len(shared), 1)
+    halo_count, share_count = max(len(halos), 1), max(len(shared) + len(windows), 1)
     return pl.pallas_call(
-        functools.partial(exchange_kernel, [m for _, m in halos], len(shared)),
+        functools.partial(exchange_kernel, [m for _, m in halos], len(shared), len(windows)),
         out_shape=shapes,
         in_specs=[vmem] * total,
         out_specs=[vmem] * len(shapes),
@@ -407,7 +502,7 @@
         compiler_params=pltpu.CompilerParams(
             collective_id=number, has_side_effects=True, vmem_limit_bytes=LIMIT
         ),
-    )(*[a for a, _ in halos], *shared)
+    )(*[a for a, _ in halos], *shared, *windows)
 
 
 def local(kernel, shapes, args, scalars, scratch):
@@ -443,37 +538,45 @@
     sized = lambda *shape: jax.ShapeDtypeStruct(shape, F32)
     row = lambda bias: bias.reshape(1, -1)
     code_block = jnp.pad(parent_codes.reshape(1, -1), ((0, 7), (0, 128 - count)))
-    left, right, codes = exchange([(x, HALO)], [code_block], 1)
+    members = lax.axis_size("dev")
+    flat = (FINE_ROWS // 2, 2 * channels)
+    (packed,) = local(pack_kernel, [sized(count, *flat)], [x], (), [])
+    left, right, codes = exchange([(packed, HALO)], [code_block], [], 1)
     codes = codes.reshape(-1, 128)
-    hidden, pooled = local(
+    hidden, packed, pooled = local(
         first_kernel,
-        [sized(count, VOX // 2, 2 * channels), sized(count, OCT // 2, 2 * channels)],
+        [
+            sized(count, VOX // 2, 2 * channels),
+            sized(count, *flat),
+            sized(count, OCT // 2, 2 * channels),
+        ],
         [x, left, right, fine_links, in_weight, row(in_bias)],
         (3,),
         conv_scratch(count + 2 * HALO, channels),
     )
-    hidden_left, hidden_right, pooled = exchange([(hidden, HALO)], [pooled], 2)
-    (first,) = local(
+    hidden_left, hidden_right, pooled = exchange([(packed, HALO)], [pooled], [], 2)
+    first, packed = local(
         second_kernel,
-        [sized(slots, VOX, wide)],
+        [sized(slots, VOX, wide), sized(slots, COARSE_ROWS, wide)],
         [pooled, codes, coarse_links, down, one_weight, row(one_bias)],
         (1, 2),
         [pltpu.VMEM((3 * slots * 8, OCT, channels), F32)] + conv_scratch(3 * slots, wide),
     )
-    first_left, first_right = exchange([(first, slots)], [], 3)
-    (lifted,) = local(
+    first_left, first_right = exchange([(packed, slots)], [], [], 3)
+    (wanted,) = local(
         third_kernel,
-        [sized(slots * 8, OCT // 2, 2 * channels)],
-        [first, first_left, first_right, coarse_links, two_weight, row(two_bias), up],
-        (3,),
-        conv_scratch(3 * slots, wide),
+        [sized(members * count + 2 * HALO, OCT // 2, 2 * channels)],
+        [first, first_left, first_right, coarse_links, codes, two_weight, row(two_bias), up],
+        (3, 4),
+        [pltpu.VMEM((slots * 8, OCT // 2, 2 * channels), F32)] + conv_scratch(3 * slots, wide),
     )
-    (lifted,) = exchange([], [lifted], 4)
+    window, low, high = exchange([], [], [wanted], 4)
     (out,) = local(
         fourth_kernel,
         [sized(count, channels, VOX)],
-        [x, hidden, hidden_left, hidden_right, lifted, codes, fine_links, out_weight, row(out_bias)],
-        (5, 6),
+        [x, hidden, hidden_left, hidden_right, window, low, high, fine_links, out_weight,
+         row(out_bias)],
+        (7,),
         conv_scratch(count + 2 * HALO, channels),
     )
     return out

time: 146 us -> 116 us (0.79)
  Pallas kernels: 143 us -> 113 us
    pallas_call x4, Pallas kernels: 96.2 us -> 60.9 us  [exchange(): pl.pallas_call(functools.partial(exchange_kernel, [m for _, m in halos],...]
    pallas_call x4 -> x5, Pallas kernels: 47 us -> 52 us  [local(): pl.pallas_call(kernel, out_shape=shapes, in_specs=[smem if i in scalars e...]
where the time goes in v2:
time: 116 us
  Pallas kernels  113 us (97%)
  local copies, waits for them, and re-layouts  2.72 us (2%)
    pallas_call x4, Pallas kernels, exchange(): pl.pallas_call(functools.partial(exchange_kernel, [m for _, m in halos],...  60.9 us
    pallas_call x5, Pallas kernels, local(): pl.pallas_call(kernel, out_shape=shapes, in_specs=[smem if i in scalars e...  52 us

profile of v2, /device:TPU:9, one launch (start us, length us, event | category | flops | bytes accessed | tf_op | source)
XLA Modules:
  0.0 115.6 jit_solution(14516245155668701408)
XLA Ops:
  0.0 1.3 %pad.4.refs_1_ = s32[8,128]{1,0:T(8,128)} pad(s32[1,4]{1,0:T(1,128)} %bitcast.10, s32[]{:T(128)} %constant.0.clone.1), padding=0_7x0_124 | pad | bytes 4116 | tf_op jit(solution)/shard_map/jit(_pad)/pad | solution.py:540
  1.3 1.5 %copy.15.down = f32[128,64]{1,0:T(8,128)} copy(f32[128,64]{0,1:T(8,128)} %param.20) | data formatting | bytes 65536 | tf_op args[6]
  2.7 2.6 %pack_kernel.1.refs_0_ = f32[4,152,128]{2,1,0:T(8,128)} custom-call(f32[4,64,512]{2,1,0:T(8,128)} %x.7), custom_call_target="tpu_custom_call" | custom-call | tf_op jit(solution)/shard_map/pack_kernel/pallas_call | solution.py:511
  5.4 12.5 %exchange_1.1 = (f32[2,152,128]{2,1,0:T(8,128)}, f32[2,152,128]{2,1,0:T(8,128)}, s32[12,8,128]{2,1,0:T(8,128)}) custom-call(f32[4,152,128]{2,1,0:T(8,128)} %pack_kernel.1.refs_0_, s32[8,128]{1,0:T(8,128)} %pad.4.refs_1_), custom_call_target="tpu_custom_call" | custom-call | tf_op jit(solution)/shard_map/exchange_1/pallas_call | solution.py:490
  17.8 11.6 %first_kernel.1 = (f32[4,256,128]{2,1,0:T(8,128)}, f32[4,152,128]{2,1,0:T(8,128)}, f32[4,32,128]{2,1,0:T(8,128)}) custom-call(f32[4,64,512]{2,1,0:T(8,128)} %x.7, f32[2,152,128]{2,1,0:T(8,128)} %get-tuple-element.21.left, f32[2,152,128]{2,1,0:T(8,128)} %get-tuple-element.22.right, s32[4,26]{1,0:T(4,128)} %links.7, f32[64,1728]{1,0:T(8,128)} %weight.4, ...), custom_call_target="tpu_custom_call" | custom-call | tf_op jit(solution)/shard_map/first_kernel/pallas_call | solution.py:511
  29.4 16.8 %exchange_2.1 = (f32[2,152,128]{2,1,0:T(8,128)}, f32[2,152,128]{2,1,0:T(8,128)}, f32[12,4,32,128]{3,2,1,0:T(8,128)}) custom-call(f32[4,152,128]{2,1,0:T(8,128)} %get-tuple-element.24.refs_0_, f32[4,32,128]{2,1,0:T(8,128)} %get-tuple-element.25.refs_1_), custom_call_target="tpu_custom_call" | custom-call | tf_op jit(solution)/shard_map/exchange_2/pallas_call | solution.py:490
  46.2 14.6 %second_kernel.1 = (f32[2,512,128]{2,1,0:T(8,128)}, f32[2,296,128]{2,1,0:T(8,128)}) custom-call(f32[12,4,32,128]{3,2,1,0:T(8,128)} %get-tuple-element.28.pooled, s32[96,128]{1,0:T(8,128)} %bitcast.6, s32[2,26]{1,0:T(2,128)} %links.6, f32[128,64]{1,0:T(8,128)} %copy.15.down, f32[128,3456]{1,0:T(8,128)} %weight.5, f32[1,128]{1,0:T(1,128)} %bitcast.11), custom_call_target="tpu_custom_call" | custom-call | tf_op jit(solution)/shard_map/second_kernel/pallas_call | solution.py:511
  60.8 18.2 %exchange_3.1 = (f32[2,296,128]{2,1,0:T(8,128)}, f32[2,296,128]{2,1,0:T(8,128)}) custom-call(f32[2,296,128]{2,1,0:T(8,128)} %get-tuple-element.31.refs_0_), custom_call_target="tpu_custom_call" | custom-call | tf_op jit(solution)/shard_map/exchange_3/pallas_call | solution.py:490
  79.0 11.1 %third_kernel.1.refs_0_ = f32[20,32,128]{2,1,0:T(8,128)} custom-call(f32[2,512,128]{2,1,0:T(8,128)} %get-tuple-element.30.first, f32[2,296,128]{2,1,0:T(8,128)} %get-tuple-element.32.left, f32[2,296,128]{2,1,0:T(8,128)} %get-tuple-element.33.right, s32[2,26]{1,0:T(2,128)} %links.6, s32[96,128]{1,0:T(8,128)} %bitcast.7, f32[128,3456]{1,0:T(8,128)} %weight.6, ...), custom_call_target="tpu_custom_call" | custom-call | tf_op jit(solution)/shard_map/third_kernel/pallas_call | solution.py:511
  90.1 13.4 %exchange_4.1 = (f32[4,8,32,128]{3,2,1,0:T(8,128)}, f32[4,2,32,128]{3,2,1,0:T(8,128)}, f32[4,2,32,128]{3,2,1,0:T(8,128)}) custom-call(f32[20,32,128]{2,1,0:T(8,128)} %third_kernel.1.refs_0_), custom_call_target="tpu_custom_call" | custom-call | tf_op jit(solution)/shard_map/exchange_4/pallas_call | solution.py:490
  103.5 12.1 %fourth_kernel.1 = f32[4,64,512]{2,1,0:T(8,128)} custom-call(f32[4,64,512]{2,1,0:T(8,128)} %x.7, f32[4,256,128]{2,1,0:T(8,128)} %get-tuple-element.23.hidden, f32[2,152,128]{2,1,0:T(8,128)} %get-tuple-element.26.left, f32[2,152,128]{2,1,0:T(8,128)} %get-tuple-element.27.right, f32[4,8,32,128]{3,2,1,0:T(8,128)} %get-tuple-element.34.window, ...), custom_call_target="tpu_custom_call" | custom-call | tf_op jit(solution)/shard_map/fourth_kernel/pallas_call | solution.py:511

commit v3 on v2

--- a/solution.py
+++ b/solution.py
@@ -39,9 +39,9 @@
 
 
 def precise(a, b, dims=((1,), (1,))):
-    return lax.dot_general(
-        a, b, (dims, ((), ())), preferred_element_type=F32, precision=lax.Precision.HIGHEST
-    )
+    (a_high, a_low), (b_high, b_low) = split(a), split(b)
+    a_high, a_low, b_high, b_low = (v.astype(BF16) for v in (a_high, a_low, b_high, b_low))
+    return product(a_high, b_high, dims) + product(a_low, b_high, dims) + product(a_high, b_low, dims)
 
 
 def spread(v):
@@ -243,7 +243,7 @@
 
     def base(slot, carry):
         piece = pieces[pl.ds(slot * 8, 8)].reshape(VOX, pieces.shape[-1])
-        lifted = precise(piece, down[...])
+        lifted = precise(piece, down[...], ((1,), (0,)))
         high, low = split(lifted)
         both = jnp.concatenate([high, low], axis=1).astype(BF16)
         parts[slot] = product(order, both, ((1,), (0,))).reshape(SIDE, SIDE, SIDE, both.shape[1])
@@ -558,7 +558,7 @@
     first, packed = local(
         second_kernel,
         [sized(slots, VOX, wide), sized(slots, COARSE_ROWS, wide)],
-        [pooled, codes, coarse_links, down, one_weight, row(one_bias)],
+        [pooled, codes, coarse_links, down.T, one_weight, row(one_bias)],
         (1, 2),
         [pltpu.VMEM((3 * slots * 8, OCT, channels), F32)] + conv_scratch(3 * slots, wide),
     )

time: 116 us -> 113 us (0.974)
  Pallas kernels: 113 us -> 111 us
  local copies, waits for them, and re-layouts: 2.72 us -> 1.25 us
    pallas_call x5, Pallas kernels: 52 us -> 50.2 us  [local(): pl.pallas_call(kernel, out_shape=shapes, in_specs=[smem if i in scalars e...]
    unnamed x1 -> x0, local copies, waits for them, and re-layouts: 1.47 us -> none
where the time goes in v3:
time: 113 us; the launch traced here: 112 us
  Pallas kernels  111 us (98%)
  local copies, waits for them, and re-layouts  1.25 us (1%)
    pallas_call x4, Pallas kernels, exchange(): pl.pallas_call(functools.partial(exchange_kernel, [m for _, m in halos],...  60.9 us
    pallas_call x5, Pallas kernels, local(): pl.pallas_call(kernel, out_shape=shapes, in_specs=[smem if i in scalars e...  50.2 us

profile of v3, /device:TPU:9, one launch (start us, length us, event | category | flops | bytes accessed | tf_op | source)
XLA Modules:
  0.0 112.4 jit_solution(14568449046511902275)
XLA Ops:
  0.0 1.3 %pad.4.refs_1_ = s32[8,128]{1,0:T(8,128)} pad(s32[1,4]{1,0:T(1,128)} %bitcast.12, s32[]{:T(128)} %constant.0.clone.1), padding=0_7x0_124 | pad | bytes 4116 | tf_op jit(solution)/shard_map/jit(_pad)/pad | solution.py:540
  1.3 2.6 %pack_kernel.1.refs_0_ = f32[4,152,128]{2,1,0:T(8,128)} custom-call(f32[4,64,512]{2,1,0:T(8,128)} %x.7), custom_call_target="tpu_custom_call" | custom-call | tf_op jit(solution)/shard_map/pack_kernel/pallas_call | solution.py:511
  3.9 12.5 %exchange_1.1 = (f32[2,152,128]{2,1,0:T(8,128)}, f32[2,152,128]{2,1,0:T(8,128)}, s32[12,8,128]{2,1,0:T(8,128)}) custom-call(f32[4,152,128]{2,1,0:T(8,128)} %pack_kernel.1.refs_0_, s32[8,128]{1,0:T(8,128)} %pad.4.refs_1_), custom_call_target="tpu_custom_call" | custom-call | tf_op jit(solution)/shard_map/exchange_1/pallas_call | solution.py:490
  16.4 11.6 %first_kernel.1 = (f32[4,256,128]{2,1,0:T(8,128)}, f32[4,152,128]{2,1,0:T(8,128)}, f32[4,32,128]{2,1,0:T(8,128)}) custom-call(f32[4,64,512]{2,1,0:T(8,128)} %x.7, f32[2,152,128]{2,1,0:T(8,128)} %get-tuple-element.21.left, f32[2,152,128]{2,1,0:T(8,128)} %get-tuple-element.22.right, s32[4,26]{1,0:T(4,128)} %links.7, f32[64,1728]{1,0:T(8,128)} %weight.4, ...), custom_call_target="tpu_custom_call" | custom-call | tf_op jit(solution)/shard_map/first_kernel/pallas_call | solution.py:511
  27.9 16.8 %exchange_2.1 = (f32[2,152,128]{2,1,0:T(8,128)}, f32[2,152,128]{2,1,0:T(8,128)}, f32[12,4,32,128]{3,2,1,0:T(8,128)}) custom-call(f32[4,152,128]{2,1,0:T(8,128)} %get-tuple-element.24.refs_0_, f32[4,32,128]{2,1,0:T(8,128)} %get-tuple-element.25.refs_1_), custom_call_target="tpu_custom_call" | custom-call | tf_op jit(solution)/shard_map/exchange_2/pallas_call | solution.py:490
  44.8 13.4 %second_kernel.1 = (f32[2,512,128]{2,1,0:T(8,128)}, f32[2,296,128]{2,1,0:T(8,128)}) custom-call(f32[12,4,32,128]{3,2,1,0:T(8,128)} %get-tuple-element.28.pooled, s32[96,128]{1,0:T(8,128)} %bitcast.7, s32[2,26]{1,0:T(2,128)} %links.6, f32[64,128]{1,0:T(8,128)} %bitcast.9, f32[128,3456]{1,0:T(8,128)} %weight.5, f32[1,128]{1,0:T(1,128)} %bitcast.13), custom_call_target="tpu_custom_call" | custom-call | tf_op jit(solution)/shard_map/second_kernel/pallas_call | solution.py:511
  58.1 18.3 %exchange_3.1 = (f32[2,296,128]{2,1,0:T(8,128)}, f32[2,296,128]{2,1,0:T(8,128)}) custom-call(f32[2,296,128]{2,1,0:T(8,128)} %get-tuple-element.31.refs_0_), custom_call_target="tpu_custom_call" | custom-call | tf_op jit(solution)/shard_map/exchange_3/pallas_call | solution.py:490
  76.4 10.6 %third_kernel.1.refs_0_ = f32[20,32,128]{2,1,0:T(8,128)} custom-call(f32[2,512,128]{2,1,0:T(8,128)} %get-tuple-element.30.first, f32[2,296,128]{2,1,0:T(8,128)} %get-tuple-element.32.left, f32[2,296,128]{2,1,0:T(8,128)} %get-tuple-element.33.right, s32[2,26]{1,0:T(2,128)} %links.6, s32[96,128]{1,0:T(8,128)} %bitcast.8, f32[128,3456]{1,0:T(8,128)} %weight.6, ...), custom_call_target="tpu_custom_call" | custom-call | tf_op jit(solution)/shard_map/third_kernel/pallas_call | solution.py:511
  87.0 13.3 %exchange_4.1 = (f32[4,8,32,128]{3,2,1,0:T(8,128)}, f32[4,2,32,128]{3,2,1,0:T(8,128)}, f32[4,2,32,128]{3,2,1,0:T(8,128)}) custom-call(f32[20,32,128]{2,1,0:T(8,128)} %third_kernel.1.refs_0_), custom_call_target="tpu_custom_call" | custom-call | tf_op jit(solution)/shard_map/exchange_4/pallas_call | solution.py:490
  100.3 12.2 %fourth_kernel.1 = f32[4,64,512]{2,1,0:T(8,128)} custom-call(f32[4,64,512]{2,1,0:T(8,128)} %x.7, f32[4,256,128]{2,1,0:T(8,128)} %get-tuple-element.23.hidden, f32[2,152,128]{2,1,0:T(8,128)} %get-tuple-element.26.left, f32[2,152,128]{2,1,0:T(8,128)} %get-tuple-element.27.right, f32[4,8,32,128]{3,2,1,0:T(8,128)} %get-tuple-element.34.window, ...), custom_call_target="tpu_custom_call" | custom-call | tf_op jit(solution)/shard_map/fourth_kernel/pallas_call | solution.py:511
